TPU v7x, 32 devices: a whole 2x2x4 slice. The times are simulated.
32 devices in a mesh: src: 8 (over z, core), tgt: 4 (over y, x).
Axes of the slice: x: 2, y: 2, z: 4, core: 2. Of those that a mesh axis runs over, the one named last changes fastest.
Arguments:
- charges: bfloat16 [65536, 64], P(('src', 'tgt')), may hold values from -6 to 6
- near_tiles: bfloat16 [4096, 128, 128], P(('src', 'tgt')), may hold values from -0.0625 to 0.0625
- near_tgt: int32 [4096], P(('src', 'tgt')), may hold values from 0 to 127
- near_src: int32 [4096], P(('src', 'tgt')), may hold values from 0 to 15
- leaf_basis: bfloat16 [512, 64, 128], P(('src', 'tgt')), may hold values from -0.125 to 0.125
- transfer: float32 [8, 3, 64, 128], P('src'), may hold values from -0.5 to 0.5
- coupling: bfloat16 [8, 512, 64, 256], P('src', 'tgt'), may hold values from -0.375 to 0.375
- far_node: int32 [8, 512, 4], P('src', 'tgt'), may hold values from 0 to 6
- target_basis: bfloat16 [512, 64, 128], P('tgt'), may hold values from -0.25 to 0.25
Outputs:
- potential: bfloat16 [65536, 64], P('tgt')
All inputs are finite; a program needn't handle non-finite values.
Results may differ from a plain program's by a relative error of at most 0.0057.
Values may be sent and summed in bfloat16 or wider, within the bound.
No kernel may reach another device: no remote copies, remote signals or barrier semaphores. Data moves between devices by JAX's collectives and lax.ppermute only.
A program may use at most 128 MiB of HBM per device.

v0:
```python
import jax
import jax.numpy as jnp
from jax import lax
from jax.sharding import PartitionSpec as P


def climb(edges, leaves):
    levels = [leaves]
    level = leaves
    width = leaves.shape[0]
    while width > 1:
        width = width // 2
        edge_slab = edges[width - 1 : 2 * width - 1]
        pairs = level.reshape(width, 2 * level.shape[1], level.shape[2])
        level = jnp.einsum("prc,pcn->prn", edge_slab, pairs, precision=lax.Precision.HIGHEST)
        levels.insert(0, level)
    return jnp.concatenate(levels, axis=0)


def shards(
    charges, near_tiles, near_tgt, near_src, leaf_basis, transfer, coupling, far_node, target_basis
):
    groups = lax.axis_size("tgt")
    tile = near_tiles.shape[1]
    slots = near_tiles.shape[0] // groups
    nrhs = charges.shape[1]
    tdev = leaf_basis.shape[0]
    tgt_tiles = target_basis.shape[0]
    local_leaves = charges.reshape(tdev, tile, nrhs)
    block_x = lax.all_gather(charges, "tgt", axis=0, tiled=True)
    block_leaves = block_x.reshape(groups * tdev, tile, nrhs)
    got_tiles, got_tgt, got_src = (
        lax.all_to_all(
            near_tiles.reshape(groups, slots, tile, tile),
            "tgt",
            split_axis=0,
            concat_axis=0,
            tiled=True,
        ),
        lax.all_to_all(
            near_tgt.reshape(groups, slots), "tgt", split_axis=0, concat_axis=0, tiled=True
        ),
        lax.all_to_all(
            near_src.reshape(groups, slots), "tgt", split_axis=0, concat_axis=0, tiled=True
        ),
    )
    sender = jnp.arange(groups, dtype=jnp.int32)[:, None] * tdev
    picked = block_leaves[(got_src + sender).reshape(-1)]
    products = jnp.einsum(
        "kab,kbn->kan",
        got_tiles.reshape(groups * slots, tile, tile),
        picked,
        preferred_element_type=jnp.float32,
    ).astype(jnp.bfloat16)
    results = products.reshape(groups * slots, tile * nrhs)
    onehot = (
        got_tgt.reshape(-1)[None, :] == jnp.arange(tgt_tiles, dtype=jnp.int32)[:, None]
    ).astype(jnp.bfloat16)
    near_part = jnp.dot(onehot, results, preferred_element_type=jnp.float32).reshape(
        tgt_tiles, tile, nrhs
    )
    own_root = jnp.einsum(
        "irp,ipn->rn", leaf_basis, local_leaves, preferred_element_type=jnp.float32
    )
    roots = lax.all_gather(own_root[None], "tgt", axis=0, tiled=True)
    table_b = climb(transfer[0], roots).astype(jnp.bfloat16)
    chosen = table_b[far_node[0]]
    stacked = chosen.reshape(chosen.shape[0], chosen.shape[1] * chosen.shape[2], chosen.shape[3])
    zed = jnp.einsum(
        "trc,tcn->trn", coupling[0], stacked, preferred_element_type=jnp.float32
    ).astype(jnp.bfloat16)
    far_part = jnp.einsum("trp,trn->tpn", target_basis, zed, preferred_element_type=jnp.float32)
    total = lax.psum(near_part + far_part, "src")
    return total.reshape(tgt_tiles * tile, nrhs).astype(jnp.bfloat16)


def solution(mesh):
    in_specs = (
        P(("src", "tgt"), None),
        P(("src", "tgt"), None, None),
        P(("src", "tgt")),
        P(("src", "tgt")),
        P(("src", "tgt"), None, None),
        P("src", None, None, None),
        P("src", "tgt", None, None),
        P("src", "tgt", None),
        P("tgt", None, None),
    )
    out_specs = P("tgt", None)
    return jax.shard_map(shards, mesh=mesh, in_specs=in_specs, out_specs=out_specs, check_vma=False)
```

profile of v0, /device:TPU:0, one launch (start us, length us, event | category | flops | bytes accessed | tf_op | source)
XLA Modules:
  0.0 229.9 jit_solution(22342178664808645)
XLA Ops:
  6.5 1.5 all_to_all.19
  8.0 5.2 %all-to-all-start.1 = ((s32[4,1,32]{2,1,0:T(1,128)}), s32[4,1,32]{2,1,0:T(1,128)S(1)}, u32[]{:S(2)}, u32[]{:S(2)}) async-start(s32[4,1,32]{2,1,0:T(1,128)} %bitcast.2), calls=%async_computation.1 | async-start | bytes 4096 | tf_op jit(solution)/shard_map/all_to_all | solution.py:43
  13.2 0.7 all_to_all.17
  13.9 3.8 %all-to-all-done.1 = s32[4,1,32]{2,1,0:T(1,128)S(1)} async-done(((s32[4,1,32]{2,1,0:T(1,128)}), s32[4,1,32]{2,1,0:T(1,128)S(1)}, u32[]{:S(2)}, u32[]{:S(2)}) %all-to-all-start.1) | async-done | bytes 544 | tf_op jit(solution)/shard_map/all_to_all | solution.py:43
  17.7 7.0 %all_to_all.26 = s32[4,1,32]{2,1,0:T(1,128)S(1)} all-to-all(s32[4,1,32]{2,1,0:T(1,128)S(1)} %bitcast.80), channel_id=1, replica_groups=mesh['src'=8,'tgt'=4] {'tgt'}, dimensions={0} | all-to-all | bytes 1024 | tf_op jit(solution)/shard_map/all_to_all | solution.py:40
  24.7 5.1 %all-to-all-start.2 = ((bf16[4,32,128,128]{3,2,1,0:T(8,128)(2,1)}), bf16[4,32,128,128]{3,2,1,0:T(8,128)(2,1)}, u32[]{:S(2)}, u32[]{:S(2)}) async-start(bf16[4,32,128,128]{3,2,1,0:T(8,128)(2,1)} %bitcast.77), calls=%async_computation.2 | async-start | bytes 8388608 | tf_op jit(solution)/shard_map/all_to_all | solution.py:33
  29.8 0.7 all-gather.3.cloned.1.call-update
  30.5 0.2 convolution_bitcast_fusion.1
  30.8 56.5 %all-gather = f32[256,64]{1,0:T(8,128)S(1)} all-gather(f32[64,64]{1,0:T(8,128)S(1)} %convolution_bitcast_fusion.1), channel_id=2, replica_groups=mesh['src'=8,'tgt'=4] {'tgt'}, dimensions={0}, use_global_device_ids=true | all-gather | bytes 81920 | tf_op jit(solution)/shard_map/all_gather | solution.py:65
  87.3 0.4 fusion.20
  87.9 0.2 fusion.9
  88.3 0.1 copy.67
  88.4 0.1 reshape.129
  88.7 13.5 %gather_fusion.1 = bf16[512,64,64]{2,1,0:T(8,128)(2,1)} fusion(bf16[7,64,64]{2,1,0:T(8,128)(2,1)S(1)} %pad_maximum_fusion, s32[1024]{0:T(1024)S(1)} %pad_clamp_fusion), kind=kCustom, calls=%fused_computation.1 | custom fusion | bytes 8390656 | tf_op jit(solution)/shard_map/gather | solution.py:67
  102.2 10.1 %fusion.3 = f32[128,64,128]{2,1,0:T(8,128)} fusion(bf16[128,64,128]{2,1,0:T(8,128)(2,1)S(1)} %copy-done, bf16[128,256,64]{2,1,0:T(8,128)(2,1)} %bitcast.75, bf16[1,128,64,256]{3,2,1,0:T(8,128)(2,1)} %param.15), kind=kOutput, calls=%fused_computation.7 | convolution fusion | flops 403177472 | bytes 14680064 | tf_op jit(solution)/shard_map/trp,trn->tpn/dot_general | solution.py:72
  112.2 0.5 broadcast.53
  112.8 0.7 reduce.6
  113.5 0.7 reduce.7
  114.3 1.5 copy_bitcast_fusion.1
  115.8 2.1 gather_fusion
  118.0 5.9 %convert_bitcast_fusion = bf16[128,64,128]{0,1,2:T(8,128)(2,1)S(1)} fusion(bf16[128,128,64]{1,2,0:T(8,128)(2,1)} %gather_fusion, bf16[128,128,128]{2,1,0:T(8,128)(2,1)} %bitcast.5), kind=kOutput, calls=%fused_computation.9 | convolution fusion | flops 269484032 | bytes 8388608 | tf_op jit(solution)/shard_map/kab,kbn->kan/dot_general | solution.py:49
  123.9 5.8 %bitcast_add_fusion = f32[128,128,64]{1,0,2:T(8,128)} fusion(f32[128,64,128]{2,1,0:T(8,128)S(1)} %copy-done.1, bf16[128,64,128]{0,1,2:T(8,128)(2,1)S(1)} %convert_bitcast_fusion, s32[128]{0:T(128)S(1)} %eq.15), kind=kOutput, calls=%fused_computation.2 | convolution fusion | flops 269500416 | bytes 10486272 | tf_op jit(solution)/shard_map/dot_general | solution.py:59
  129.7 89.2 %all-reduce.1 = bf16[128,128,64]{1,0,2:T(8,128)(2,1)} all-reduce(f32[128,128,64]{1,0,2:T(8,128)} %bitcast_add_fusion), channel_id=1, replica_groups=mesh['src'=8,'tgt'=4] {'src'}, use_global_device_ids=true, to_apply=%region_0.0 | all-reduce | flops 1048576 | bytes 6291456 | tf_op jit(solution)/shard_map/psum | solution.py:73
  218.8 4.3 %copy.87 = bf16[8,8,128,128]{3,1,2,0:T(8,128)(2,1)} copy(bf16[8,8,128,128]{3,2,1,0:T(8,128)(2,1)} %bitcast.76) | data formatting | bytes 4194304
  (30 shorter events, 0.8 us)
Async XLA Ops:
  6.5 95.6 %copy-start = (bf16[128,64,128]{2,1,0:T(8,128)(2,1)S(1)}, bf16[128,64,128]{2,1,0:T(8,128)(2,1)}, u32[]{:S(2)}) copy-start(bf16[128,64,128]{2,1,0:T(8,128)(2,1)} %param.17) | copy-start | bytes 6291460
  8.0 9.7 %all-to-all-start.1 = ((s32[4,1,32]{2,1,0:T(1,128)}), s32[4,1,32]{2,1,0:T(1,128)S(1)}, u32[]{:S(2)}, u32[]{:S(2)}) async-start(s32[4,1,32]{2,1,0:T(1,128)} %bitcast.2), calls=%async_computation.1 | async-start | bytes 4096 | tf_op jit(solution)/shard_map/all_to_all | solution.py:43
  24.7 5.8 %copy-start.2 = (bf16[2048,64]{0,1:T(8,128)(2,1)S(1)}, bf16[2048,64]{0,1:T(8,128)(2,1)}, u32[]{:S(2)}) copy-start(bf16[2048,64]{0,1:T(8,128)(2,1)} %param.9) | copy-start | bytes 786436
  24.7 5.8 %copy-start.3 = (bf16[16,64,128]{2,1,0:T(8,128)(2,1)S(1)}, bf16[16,64,128]{2,1,0:T(8,128)(2,1)}, u32[]{:S(2)}) copy-start(bf16[16,64,128]{2,1,0:T(8,128)(2,1)} %param.13) | copy-start | bytes 786436
  24.7 62.6 %copy-start.4 = (f32[1,3,64,128]{3,2,1,0:T(8,128)S(1)}, f32[1,3,64,128]{3,2,1,0:T(8,128)}, u32[]{:S(2)}) copy-start(f32[1,3,64,128]{3,2,1,0:T(8,128)} %param.14) | copy-start | bytes 294916
  24.7 63.1 %copy-start.5 = (s32[1,128,4]{1,2,0:T(4,128)S(1)}, s32[1,128,4]{1,2,0:T(4,128)}, u32[]{:S(2)}) copy-start(s32[1,128,4]{1,2,0:T(4,128)} %param.16) | copy-start | bytes 6148
  24.7 93.2 %all-to-all-start.2 = ((bf16[4,32,128,128]{3,2,1,0:T(8,128)(2,1)}), bf16[4,32,128,128]{3,2,1,0:T(8,128)(2,1)}, u32[]{:S(2)}, u32[]{:S(2)}) async-start(bf16[4,32,128,128]{3,2,1,0:T(8,128)(2,1)} %bitcast.77), calls=%async_computation.2 | async-start | bytes 8388608 | tf_op jit(solution)/shard_map/all_to_all | solution.py:33
  29.8 84.5 %all-gather.3.cloned.1.call-start = ((), (), s32[]{:S(2)}) async-start(), calls=%async_computation.3 | async-start | bytes 1310720 | tf_op jit(solution)/shard_map/all_gather | solution.py:30
  118.0 5.9 %copy-start.1 = (f32[128,64,128]{2,1,0:T(8,128)S(1)}, f32[128,64,128]{2,1,0:T(8,128)}, u32[]{:S(2)}) copy-start(f32[128,64,128]{2,1,0:T(8,128)} %fusion.3) | copy-start | bytes 12582916
Sparse Core Ops, SparseCore 0:
  32.5 44.3 all-gather.2
where the time goes:
time: 230 us
  blocking collectives  153 us (67%)
  local copies, waits for them, and re-layouts  25 us (11%)
  matrix products  22.5 us (10%)
  between operations  13.6 us (6%)
  starting transfers between devices  10.3 us (4%)
  waiting for transfers between devices  4.54 us (2%)
    psum x1, blocking collectives, shards(): total = lax.psum(near_part + far_part, 'src')  89.2 us
    all_gather x1, blocking collectives, shards(): roots = lax.all_gather(own_root[None], 'tgt', axis=0, tiled=True)  56.5 us
    gather x1, local copies, waits for them, and re-layouts, shards(): chosen = table_b[far_node[0]]  13.5 us
    dot_general x1, matrix products, shards(): jnp.einsum('trp,trn->tpn', target_basis, zed, preferred_element_type=jnp....  10.1 us
    all_to_all x1, blocking collectives, shards(): lax.all_to_all(near_tgt.reshape(groups, slots), 'tgt', split_axis=0, conc...  6.97 us
    dot_general x1, matrix products, shards(): jnp.einsum('kab,kbn->kan', got_tiles.reshape(groups * slots, tile, tile),...  5.94 us
    dot_general x1, matrix products, shards(): jnp.dot(onehot, results, preferred_element_type=jnp.float32)  5.76 us
    all_to_all x1, starting transfers between devices, shards(): lax.all_to_all(near_src.reshape(groups, slots), 'tgt', split_axis=0, conc...  5.16 us
  transfers between devices with their start and end apart: 3, of which 1 were waited for; matrix products, arithmetic and copies ran while one was open for 13% of the time, Pallas kernels for 0%

commit v1 on v0

--- a/solution.py
+++ b/solution.py
@@ -70,7 +70,7 @@
         "trc,tcn->trn", coupling[0], stacked, preferred_element_type=jnp.float32
     ).astype(jnp.bfloat16)
     far_part = jnp.einsum("trp,trn->tpn", target_basis, zed, preferred_element_type=jnp.float32)
-    total = lax.psum(near_part + far_part, "src")
+    total = jnp.sum(lax.all_gather(near_part + far_part, "src"), axis=0)
     return total.reshape(tgt_tiles * tile, nrhs).astype(jnp.bfloat16)
 
 

time: 230 us -> 444 us (1.93)
  waiting for transfers between devices: 4.54 us -> 294 us
  blocking collectives: 153 us -> 63.5 us
  other arithmetic: 1.39 us -> 15.2 us
    all_gather x0 -> x1, waiting for transfers between devices: none -> 289 us  [shards(): total = jnp.sum(lax.all_gather(near_part + far_part, 'src'), axis=0)]
    psum x1 -> x0, blocking collectives: 89.2 us -> none  [shards(): total = lax.psum(near_part + far_part, 'src')]
    reduce_sum x0 -> x1, other arithmetic: none -> 13.9 us  [shards(): total = jnp.sum(lax.all_gather(near_part + far_part, 'src'), axis=0)]
  transfers between devices with their start and end apart: 3 -> 4, of which waited for: 1 -> 2; matrix products, arithmetic and copies ran while one was open for 13% -> 7% of each run, Pallas kernels for 0% -> 0%
where the time goes in v1:
time: 444 us
  waiting for transfers between devices  294 us (66%)
  blocking collectives  63.5 us (14%)
  local copies, waits for them, and re-layouts  25 us (6%)
  matrix products  22.7 us (5%)
  other arithmetic  15.2 us (3%)
  between operations  13.6 us (3%)
  starting transfers between devices  10.3 us (2%)
    all_gather x1, waiting for transfers between devices, shards(): total = jnp.sum(lax.all_gather(near_part + far_part, 'src'), axis=0)  289 us
    all_gather x1, blocking collectives, shards(): roots = lax.all_gather(own_root[None], 'tgt', axis=0, tiled=True)  56.5 us
    reduce_sum x1, other arithmetic, shards(): total = jnp.sum(lax.all_gather(near_part + far_part, 'src'), axis=0)  13.9 us
    gather x1, local copies, waits for them, and re-layouts, shards(): chosen = table_b[far_node[0]]  13.5 us
    dot_general x1, matrix products, shards(): jnp.einsum('trp,trn->tpn', target_basis, zed, preferred_element_type=jnp....  10.1 us
  transfers between devices with their start and end apart: 4, of which 2 were waited for; matrix products, arithmetic and copies ran while one was open for 7% of the time, Pallas kernels for 0%

profile of v1, /device:TPU:0, one launch (start us, length us, event | category | flops | bytes accessed | tf_op | source)
XLA Modules:
  0.0 443.9 jit_solution(10196314517709401212)
XLA Ops:
  6.5 1.5 all_to_all.19
  8.0 5.2 %all-to-all-start.1 = ((s32[4,1,32]{2,1,0:T(1,128)}), s32[4,1,32]{2,1,0:T(1,128)S(1)}, u32[]{:S(2)}, u32[]{:S(2)}) async-start(s32[4,1,32]{2,1,0:T(1,128)} %bitcast.2), calls=%async_computation.1 | async-start | bytes 4096 | tf_op jit(solution)/shard_map/all_to_all | solution.py:43
  13.2 0.7 all_to_all.17
  13.9 3.8 all-to-all-done.1
  17.7 7.0 %all_to_all.26 = s32[4,1,32]{2,1,0:T(1,128)S(1)} all-to-all(s32[4,1,32]{2,1,0:T(1,128)S(1)} %bitcast.82), channel_id=1, replica_groups=mesh['src'=8,'tgt'=4] {'tgt'}, dimensions={0} | all-to-all | bytes 1024 | tf_op jit(solution)/shard_map/all_to_all | solution.py:40
  24.7 5.1 %all-to-all-start.2 = ((bf16[4,32,128,128]{3,2,1,0:T(8,128)(2,1)}), bf16[4,32,128,128]{3,2,1,0:T(8,128)(2,1)}, u32[]{:S(2)}, u32[]{:S(2)}) async-start(bf16[4,32,128,128]{3,2,1,0:T(8,128)(2,1)} %bitcast.79), calls=%async_computation.2 | async-start | bytes 8388608 | tf_op jit(solution)/shard_map/all_to_all | solution.py:33
  29.8 0.7 all-gather.5.cloned.1.call-update
  30.6 0.2 convolution_bitcast_fusion.1
  30.8 56.5 %all-gather = f32[256,64]{1,0:T(8,128)S(1)} all-gather(f32[64,64]{1,0:T(8,128)S(1)} %convolution_bitcast_fusion.1), channel_id=2, replica_groups=mesh['src'=8,'tgt'=4] {'tgt'}, dimensions={0}, use_global_device_ids=true | all-gather | bytes 81920 | tf_op jit(solution)/shard_map/all_gather | solution.py:65
  87.4 0.4 fusion.20
  87.9 0.1 copy.67
  88.4 0.2 fusion.9
  88.7 13.5 %gather_fusion.1 = bf16[512,64,64]{2,1,0:T(8,128)(2,1)} fusion(bf16[7,64,64]{2,1,0:T(8,128)(2,1)S(1)} %pad_maximum_fusion, s32[1024]{0:T(1024)S(1)} %pad_clamp_fusion), kind=kCustom, calls=%fused_computation.1 | custom fusion | bytes 8390656 | tf_op jit(solution)/shard_map/gather | solution.py:67
  102.2 10.1 %fusion.3 = f32[128,64,128]{2,1,0:T(8,128)} fusion(bf16[128,64,128]{2,1,0:T(8,128)(2,1)S(1)} %copy-done, bf16[128,256,64]{2,1,0:T(8,128)(2,1)} %bitcast.77, bf16[1,128,64,256]{3,2,1,0:T(8,128)(2,1)} %param.15), kind=kOutput, calls=%fused_computation.7 | convolution fusion | flops 403177472 | bytes 14680064 | tf_op jit(solution)/shard_map/trp,trn->tpn/dot_general | solution.py:72
  112.3 0.5 broadcast.53
  112.8 0.7 reduce.6
  113.5 0.7 reduce.7
  114.3 1.5 copy_bitcast_fusion.1
  115.8 2.1 gather_fusion
  118.0 5.9 %convert_bitcast_fusion = bf16[128,64,128]{0,1,2:T(8,128)(2,1)S(1)} fusion(bf16[128,128,64]{1,2,0:T(8,128)(2,1)} %gather_fusion, bf16[128,128,128]{2,1,0:T(8,128)(2,1)} %bitcast.5), kind=kOutput, calls=%fused_computation.9 | convolution fusion | flops 269484032 | bytes 8388608 | tf_op jit(solution)/shard_map/kab,kbn->kan/dot_general | solution.py:49
  123.9 5.9 %bitcast_add_fusion = f32[128,128,64]{1,0,2:T(8,128)} fusion(f32[128,64,128]{2,1,0:T(8,128)S(1)} %copy-done.2, bf16[128,64,128]{0,1,2:T(8,128)(2,1)S(1)} %convert_bitcast_fusion, s32[128]{0:T(128)S(1)} %eq.15), kind=kOutput, calls=%fused_computation.2 | convolution fusion | flops 269500416 | bytes 10486272 | tf_op jit(solution)/shard_map/dot_general | solution.py:59
  129.8 289.0 %all-gather.7.cloned.1.call-done = f32[1024,128,64]{1,0,2:T(8,128)} async-done(((f32[128,128,64]{1,0,2:T(8,128)}), f32[1024,128,64]{1,0,2:T(8,128)}) %all-gather.7.cloned.1.call-update) | async-done | bytes 33554448 | tf_op jit(solution)/shard_map/all_gather | solution.py:73
  418.9 13.9 %reduce_sum.9 = bf16[128,128,64]{1,0,2:T(8,128)(2,1)} reduce(f32[8,128,128,64]{2,1,0,3:T(8,128)} %bitcast.76, f32[]{:T(128)} %constant.3.clone.1), dimensions={0}, to_apply=%region_0.0 | reduce | flops 7340032 | bytes 35651588 | tf_op jit(solution)/shard_map/reduce_sum | solution.py:73
  432.7 4.3 copy.87
  (35 shorter events, 1.0 us)
Async XLA Ops:
  6.5 95.7 %copy-start = (bf16[128,64,128]{2,1,0:T(8,128)(2,1)S(1)}, bf16[128,64,128]{2,1,0:T(8,128)(2,1)}, u32[]{:S(2)}) copy-start(bf16[128,64,128]{2,1,0:T(8,128)(2,1)} %param.17) | copy-start | bytes 6291460
  8.0 9.7 %all-to-all-start.1 = ((s32[4,1,32]{2,1,0:T(1,128)}), s32[4,1,32]{2,1,0:T(1,128)S(1)}, u32[]{:S(2)}, u32[]{:S(2)}) async-start(s32[4,1,32]{2,1,0:T(1,128)} %bitcast.2), calls=%async_computation.1 | async-start | bytes 4096 | tf_op jit(solution)/shard_map/all_to_all | solution.py:43
  24.7 5.9 %copy-start.3 = (bf16[2048,64]{0,1:T(8,128)(2,1)S(1)}, bf16[2048,64]{0,1:T(8,128)(2,1)}, u32[]{:S(2)}) copy-start(bf16[2048,64]{0,1:T(8,128)(2,1)} %param.9) | copy-start | bytes 786436
  24.7 5.9 %copy-start.4 = (bf16[16,64,128]{2,1,0:T(8,128)(2,1)S(1)}, bf16[16,64,128]{2,1,0:T(8,128)(2,1)}, u32[]{:S(2)}) copy-start(bf16[16,64,128]{2,1,0:T(8,128)(2,1)} %param.13) | copy-start | bytes 786436
  24.7 62.6 %copy-start.6 = (s32[1,128,4]{1,2,0:T(4,128)S(1)}, s32[1,128,4]{1,2,0:T(4,128)}, u32[]{:S(2)}) copy-start(s32[1,128,4]{1,2,0:T(4,128)} %param.16) | copy-start | bytes 6148
  24.7 62.6 %copy-start.5 = (f32[1,3,64,128]{3,2,1,0:T(8,128)S(1)}, f32[1,3,64,128]{3,2,1,0:T(8,128)}, u32[]{:S(2)}) copy-start(f32[1,3,64,128]{3,2,1,0:T(8,128)} %param.14) | copy-start | bytes 294916
  24.7 93.2 %all-to-all-start.2 = ((bf16[4,32,128,128]{3,2,1,0:T(8,128)(2,1)}), bf16[4,32,128,128]{3,2,1,0:T(8,128)(2,1)}, u32[]{:S(2)}, u32[]{:S(2)}) async-start(bf16[4,32,128,128]{3,2,1,0:T(8,128)(2,1)} %bitcast.79), calls=%async_computation.2 | async-start | bytes 8388608 | tf_op jit(solution)/shard_map/all_to_all | solution.py:33
  29.8 84.5 %all-gather.5.cloned.1.call-start = ((), (), s32[]{:S(2)}) async-start(), calls=%async_computation.3 | async-start | bytes 1310720 | tf_op jit(solution)/shard_map/all_gather | solution.py:30
  30.5 388.3 %all-gather.7.cloned.1.call-start = ((), (), s32[]{:S(2)}) async-start(), calls=%async_computation.4 | async-start | bytes 37748736 | tf_op jit(solution)/shard_map/all_gather | solution.py:73
  118.0 5.9 %copy-start.2 = (f32[128,64,128]{2,1,0:T(8,128)S(1)}, f32[128,64,128]{2,1,0:T(8,128)}, u32[]{:S(2)}) copy-start(f32[128,64,128]{2,1,0:T(8,128)} %fusion.3) | copy-start | bytes 12582916
  418.9 18.1 %copy-start.1 = (bf16[128,64,128]{2,1,0:T(8,128)(2,1)S(1)}, bf16[128,64,128]{2,1,0:T(8,128)(2,1)}, u32[]{:S(2)}) copy-start(bf16[128,64,128]{2,1,0:T(8,128)(2,1)} %param.17) | copy-start | bytes 6291460
Sparse Core Ops, SparseCore 0:
  32.5 44.3 all-gather.4
  130.0 288.8 all-gather.6
